TPU v7x, 32 devices: a whole 2x2x4 slice. The times are simulated.
32 devices in a mesh: dp: 2 (over y), tensor: 8 (over z, core), fisher: 2 (over x).
Axes of the slice: x: 2, y: 2, z: 4, core: 2. Of those that a mesh axis runs over, the one named last changes fastest.
Arguments:
- train_inputs: bfloat16 [44, 257, 1280], P('dp', None, 'fisher'), may hold values from -6 to 6
- train_cotangents: bfloat16 [44, 257, 3840], P('dp', None, 'tensor'), may hold values from -6 to 6
- train_ids: int32 [44], P('dp'), may hold values from 0 to 15
- query_projection_inputs: bfloat16 [8, 257, 1280], P('tensor', None, 'fisher'), may hold values from -6 to 6
- query_output_cotangents: bfloat16 [8, 257, 3840], P('tensor'), may hold values from -6 to 6
- query_ids: int32 [8], replicated, may hold values from 0 to 15
- fisher_diagonal_weight: bfloat16 [2, 3840, 1280], P(None, 'tensor', 'fisher'), may hold values from 0.049804688 to 2
- layer_index: int32 [16], replicated, may hold values from 0 to 1
Outputs:
- influence: float32 [16, 16, 16], P(('dp', 'fisher'), None, 'tensor')
All inputs are finite; a program needn't handle non-finite values.
Results may differ from a plain program's by a relative error of at most 0.004.
Values may be sent and summed in bfloat16 or wider, within the bound.
A program may use at most 128 MiB of HBM per device.

v0:
```python
import math
import jax
import jax.numpy as jnp
from jax import lax
from jax.sharding import PartitionSpec as P

D = 1280
HEAD_DIM = 80
SEQ = 257
TID_DEV = 4
QIDS = 16


def local(
    train_inputs,
    train_cotangents,
    train_ids,
    query_projection_inputs,
    query_output_cotangents,
    query_ids,
    fisher_diagonal_weight,
    layer_index,
):
    head_width = 3 * HEAD_DIM
    scale_factor = 1.0 / (SEQ * math.sqrt(3 * HEAD_DIM * D))
    local_heads = train_cotangents.shape[2] // head_width
    count_train = train_inputs.shape[0]
    half_width = train_inputs.shape[2]
    stored_count = fisher_diagonal_weight.shape[0]
    head_first = lax.axis_index("tensor") * local_heads
    own_layers = lax.dynamic_slice_in_dim(layer_index, head_first, local_heads, 0)
    picked = own_layers[None, :] == jnp.arange(stored_count, dtype=jnp.int32)[:, None]
    stacked = fisher_diagonal_weight.reshape(stored_count, local_heads, head_width, half_width)
    chosen = jnp.sum(jnp.where(picked[:, :, None, None], stacked.astype(jnp.float32), 0.0), axis=0)
    fisher_layer = chosen.reshape(local_heads * head_width, half_width).astype(jnp.bfloat16)
    train_grad = jnp.einsum(
        "nsr,nsd->nrd", train_cotangents, train_inputs, preferred_element_type=jnp.float32
    ).astype(jnp.bfloat16)
    fisher_local = fisher_layer.astype(jnp.float32)
    received = lax.all_to_all(
        query_output_cotangents, "tensor", split_axis=2, concat_axis=0, tiled=True
    )
    block_grad = jnp.einsum(
        "kzo,kzj->koj",
        received,
        lax.all_gather(query_projection_inputs, "tensor", axis=0, tiled=True),
        preferred_element_type=jnp.float32,
    )
    weighted = (fisher_local[None] * block_grad).astype(jnp.bfloat16)
    count_query = weighted.shape[0]
    train_flat = train_grad.reshape(count_train, local_heads, head_width * half_width)
    query_flat = weighted.reshape(count_query, local_heads, head_width * half_width)
    scores = (
        lax.dot_general(
            train_flat, query_flat, (((2,), (2,)), ((1,), (1,))), preferred_element_type=jnp.float32
        )
        * scale_factor
    )
    total_ids = TID_DEV * lax.axis_size("dp") * lax.axis_size("fisher")
    train_hot = (train_ids[:, None] == jnp.arange(total_ids, dtype=jnp.int32)[None, :]).astype(
        jnp.float32
    )
    query_hot = (query_ids[:, None] == jnp.arange(QIDS, dtype=jnp.int32)[None, :]).astype(
        jnp.float32
    )
    buckets = jnp.einsum(
        "hnm,na,mb->hab", scores, train_hot, query_hot, precision=lax.Precision.HIGHEST
    )
    shares = lax.psum_scatter(buckets, ("dp", "fisher"), scatter_dimension=1, tiled=True)
    return jnp.transpose(shares, (1, 2, 0))


def solution(mesh):
    in_specs = (
        P("dp", None, "fisher"),
        P("dp", None, "tensor"),
        P("dp"),
        P("tensor", None, "fisher"),
        P("tensor", None, None),
        P(),
        P(None, "tensor", "fisher"),
        P(),
    )
    out_specs = P(("dp", "fisher"), None, "tensor")
    return jax.shard_map(local, mesh=mesh, in_specs=in_specs, out_specs=out_specs, check_vma=False)
```

profile of v0, /device:TPU:0, one launch (start us, length us, event | category | flops | bytes accessed | tf_op | source)
XLA Modules:
  0.0 169.4 jit_solution(9806941971329295735)
XLA Ops:
  6.5 0.7 all-gather.2.cloned.1.call-update
  7.3 12.2 %copy.12 = bf16[1,257,3840]{1,0,2:T(2,128)(2,1)} copy(bf16[1,257,3840]{2,1,0:T(8,128)(2,1)} %param.12) | data formatting | bytes 3947520 | tf_op args[4]
  19.5 0.5 broadcast.15
  20.0 24.6 %reduce.1 = bf16[3840,257]{1,0:T(8,128)(2,1)S(1)} reduce(bf16[3840,1,257]{2,1,0:T(2,128)(2,1)} %bitcast.29, bf16[]{:T(256)} %broadcast.15), dimensions={1}, to_apply=%bitcast.22.reduce_sub_computation | reduce | bytes 3947522
  44.6 7.1 %reshape.44 = bf16[8,2,61680]{2,1,0:T(2,128)(2,1)} reshape(bf16[3840,257]{1,0:T(8,128)(2,1)S(1)} %reduce.1) | data formatting | bytes 3947520
  51.7 6.4 %all-to-all-start = ((bf16[8,2,61680]{2,1,0:T(2,128)(2,1)}), bf16[8,2,61680]{2,1,0:T(2,128)(2,1)S(1)}, u32[]{:S(2)}, u32[]{:S(2)}) async-start(bf16[8,2,61680]{2,1,0:T(2,128)(2,1)} %reshape.44), calls=%async_computation | async-start | bytes 3948544 | tf_op jit(solution)/shard_map/all_to_all | solution.py:40
  58.2 0.1 broadcast_in_dim.24
  58.3 0.1 broadcast_in_dim.25
  58.4 1.6 select_reduce_fusion
  60.0 1.2 convert_element_type.36
  61.2 15.5 %convolution_convert_fusion = bf16[22,480,640]{2,1,0:T(8,128)(2,1)} fusion(bf16[22,257,480]{2,1,0:T(8,128)(2,1)} %param.9, bf16[22,257,640]{2,1,0:T(8,128)(2,1)} %param.8), kind=kOutput, calls=%fused_computation.2 | convolution fusion | flops 3480576000 | bytes 26181760 | tf_op jit(solution)/shard_map/nsr,nsd->nrd/dot_general | solution.py:36
  76.7 18.1 %reshape.35 = bf16[22,2,153600]{2,1,0:T(2,128)(2,1)} reshape(bf16[22,480,640]{2,1,0:T(8,128)(2,1)} %convolution_convert_fusion) | data formatting | bytes 27033600 | tf_op jit(solution)/shard_map/reshape | solution.py:51
  94.7 0.6 dynamic-slice
  96.0 8.5 %all-to-all-done = bf16[8,2,61680]{2,1,0:T(2,128)(2,1)S(1)} async-done(((bf16[8,2,61680]{2,1,0:T(2,128)(2,1)}), bf16[8,2,61680]{2,1,0:T(2,128)(2,1)S(1)}, u32[]{:S(2)}, u32[]{:S(2)}) %all-to-all-start) | async-done | bytes 1973792 | tf_op jit(solution)/shard_map/all_to_all | solution.py:40
  104.5 8.2 %reshape.45 = bf16[3840,1,257]{2,1,0:T(2,128)(2,1)} reshape(bf16[8,2,61680]{2,1,0:T(2,128)(2,1)S(1)} %all-to-all-done) | data formatting | bytes 3947520
  112.7 3.2 %copy.22 = bf16[1,257,3840]{1,2,0:T(8,128)(2,1)S(1)} copy(bf16[1,257,3840]{1,0,2:T(2,128)(2,1)} %bitcast.30) | data formatting | bytes 3947520
  115.9 2.6 %copy.14 = bf16[1,257,8,480]{3,1,2,0:T(8,128)(2,1)} copy(bf16[1,257,8,480]{1,3,2,0:T(8,128)(2,1)S(1)} %bitcast.31) | data formatting | bytes 3947520 | tf_op jit(solution)/shard_map/all_to_all | solution.py:40
  118.5 8.0 %multiply_convert_fusion = bf16[8,480,640]{2,1,0:T(8,128)(2,1)} fusion(f32[480,640]{1,0:T(8,128)} %convert_element_type.36, bf16[8,257,640]{2,1,0:T(8,128)(2,1)} %all-gather.2.cloned.1.call-done, bf16[1,257,8,480]{3,1,2,0:T(8,128)(2,1)} %copy.14), kind=kOutput, calls=%fused_computation.3 | convolution fusion | flops 1268121600 | bytes 10749440 | tf_op jit(solution)/shard_map/kzo,kzj->koj/dot_general | solution.py:43
  126.5 7.4 %reshape.36 = bf16[8,2,153600]{2,1,0:T(2,128)(2,1)} reshape(bf16[8,480,640]{2,1,0:T(8,128)(2,1)} %multiply_convert_fusion) | data formatting | bytes 9830400 | tf_op jit(solution)/shard_map/reshape | solution.py:52
  133.8 11.7 %fusion.9 = f32[22,16]{0,1:T(8,128)S(1)} fusion(bf16[8,2,153600]{2,1,0:T(2,128)(2,1)} %reshape.36, bf16[22,2,153600]{2,1,0:T(2,128)(2,1)} %reshape.35), kind=kOutput, calls=%fused_computation.10 | convolution fusion | flops 108134752 | bytes 18433408 | tf_op jit(solution)/shard_map/dot_general | solution.py:54
  145.6 0.1 convolution_bitcast_fusion.1
  145.7 0.2 convolution_bitcast_fusion
  145.9 16.0 %all-reduce = f32[2,16,16]{2,1,0:T(8,128)S(1)} all-reduce(f32[2,16,16]{2,1,0:T(8,128)S(1)} %convolution_bitcast_fusion), channel_id=2, replica_groups=mesh['dp'=2,'tensor'=8,'fisher'=2] {'dp','fisher'}, use_global_device_ids=true, to_apply=%region_1.2.clone | all-reduce | flops 512 | bytes 4096
  162.0 0.6 copy.17
  (13 shorter events, 0.1 us)
Async XLA Ops:
  6.5 111.9 %all-gather.2.cloned.1.call-start = ((), (), s32[]{:S(2)}) async-start(), calls=%async_computation.1 | async-start | bytes 3041280 | tf_op jit(solution)/shard_map/all_gather | solution.py:46
  44.6 13.5 %copy-start.1 = (s32[16]{0:T(128)S(1)}, s32[16]{0:T(128)}, u32[]{:S(2)}) copy-start(s32[16]{0:T(128)} %param.15) | copy-start | bytes 196
  51.7 52.8 %all-to-all-start = ((bf16[8,2,61680]{2,1,0:T(2,128)(2,1)}), bf16[8,2,61680]{2,1,0:T(2,128)(2,1)S(1)}, u32[]{:S(2)}, u32[]{:S(2)}) async-start(bf16[8,2,61680]{2,1,0:T(2,128)(2,1)} %reshape.44), calls=%async_computation | async-start | bytes 3948544 | tf_op jit(solution)/shard_map/all_to_all | solution.py:40
  76.7 18.1 %copy-start.3 = (u32[32]{0:T(128)S(1)}, u32[32]{0:T(128)}, u32[]{:S(2)}) copy-start(u32[32]{0:T(128)} %constant.20) | copy-start | bytes 388
  133.8 11.7 %copy-start = (s32[22]{0:T(128)S(1)}, s32[22]{0:T(128)}, u32[]{:S(2)}) copy-start(s32[22]{0:T(128)} %param.10) | copy-start | bytes 268
  133.8 11.9 %copy-start.2 = (s32[8]{0:T(128)S(1)}, s32[8]{0:T(128)}, u32[]{:S(2)}) copy-start(s32[8]{0:T(128)} %param.13) | copy-start | bytes 100
Sparse Core Ops, SparseCore 0:
  9.0 37.1 all-gather.1
where the time goes:
time: 171 us; the launch traced here: 169 us
  local copies, waits for them, and re-layouts  60.8 us (36%)
  matrix products  35.6 us (21%)
  other arithmetic  27.4 us (16%)
  blocking collectives  16 us (9%)
  between operations  14.1 us (8%)
  waiting for transfers between devices  9.24 us (5%)
  starting transfers between devices  6.37 us (4%)
    unnamed x14, local copies, waits for them, and re-layouts  31.9 us
    unnamed x1, other arithmetic  24.6 us
    reshape x1, local copies, waits for them, and re-layouts, local(): train_grad.reshape(count_train, local_heads, head_width * half_width)  18.1 us
    unnamed x1, blocking collectives  16 us
    dot_general x1, matrix products, local(): jnp.einsum('nsr,nsd->nrd', train_cotangents, train_inputs, preferred_elem...  15.5 us
    dot_general x1, matrix products, local(): lax.dot_general(train_flat, query_flat, (((2,), (2,)), ((1,), (1,))), pre...  11.7 us
    all_to_all x1, waiting for transfers between devices, local(): lax.all_to_all(query_output_cotangents, 'tensor', split_axis=2, concat_ax...  8.53 us
    dot_general x1, matrix products, local(): jnp.einsum('kzo,kzj->koj', received, lax.all_gather(query_projection_inpu...  7.99 us
  transfers between devices with their start and end apart: 2, of which 1 were waited for; matrix products, arithmetic and copies ran while one was open for 56% of the time, Pallas kernels for 0%

commit v1 on v0

--- a/solution.py
+++ b/solution.py
@@ -1,14 +1,26 @@
+import functools
 import math
 import jax
 import jax.numpy as jnp
 from jax import lax
 from jax.sharding import PartitionSpec as P
+from jax.lax import all_to_all, psum
 
 D = 1280
 HEAD_DIM = 80
 SEQ = 257
 TID_DEV = 4
 QIDS = 16
+
+
+def check_frames(row_data, which_axis):
+    return jnp.concatenate(
+        all_to_all(jnp.stack(jnp.split(row_data, psum(1, which_axis), axis=2)), which_axis, 0, 0),
+        axis=0,
+    )
+
+
+detail_ladders = functools.partial(check_frames, which_axis="tensor")
 
 
 def local(
@@ -37,9 +49,7 @@
         "nsr,nsd->nrd", train_cotangents, train_inputs, preferred_element_type=jnp.float32
     ).astype(jnp.bfloat16)
     fisher_local = fisher_layer.astype(jnp.float32)
-    received = lax.all_to_all(
-        query_output_cotangents, "tensor", split_axis=2, concat_axis=0, tiled=True
-    )
+    received = detail_ladders(query_output_cotangents)
     block_grad = jnp.einsum(
         "kzo,kzj->koj",
         received,

time: 171 us -> 144 us (0.84)
  other arithmetic: 27.4 us -> 0.4 us
  local copies, waits for them, and re-layouts: 60.8 us -> 37.5 us
  waiting for transfers between devices: 9.24 us -> 31.9 us
    unnamed x1 -> x0, other arithmetic: 24.6 us -> none
    all_to_all x1, waiting for transfers between devices: 8.53 us -> 31.2 us  [check_frames(): all_to_all(jnp.stack(jnp.split(row_data, psum(1, which_axis), axis=2)), w...]
    unnamed x14 -> x20, local copies, waits for them, and re-layouts: 31.9 us -> 10.2 us
    all_to_all x1 -> x0, local copies, waits for them, and re-layouts: 2.6 us -> none  [local(): lax.all_to_all(query_output_cotangents, 'tensor', split_axis=2, concat_ax...]
  transfers between devices with their start and end apart: 2 -> 2, of which waited for: 1 -> 1; matrix products, arithmetic and copies ran while one was open for 56% -> 32% of each run, Pallas kernels for 0% -> 0%
where the time goes in v1:
time: 144 us; the launch traced here: 143 us
  local copies, waits for them, and re-layouts  37.5 us (26%)
  matrix products  36.5 us (25%)
  waiting for transfers between devices  31.9 us (22%)
  blocking collectives  16 us (11%)
  between operations  14.1 us (10%)
  starting transfers between devices  6.49 us (5%)
    all_to_all x1, waiting for transfers between devices, check_frames(): all_to_all(jnp.stack(jnp.split(row_data, psum(1, which_axis), axis=2)), w...  31.2 us
    reshape x1, local copies, waits for them, and re-layouts, local(): train_grad.reshape(count_train, local_heads, head_width * half_width)  18.1 us
    unnamed x1, blocking collectives  16 us
    dot_general x1, matrix products, local(): jnp.einsum('nsr,nsd->nrd', train_cotangents, train_inputs, preferred_elem...  15.7 us
    dot_general x1, matrix products, local(): lax.dot_general(train_flat, query_flat, (((2,), (2,)), ((1,), (1,))), pre...  13.4 us
    unnamed x20, local copies, waits for them, and re-layouts  10.2 us
    reshape x1, local copies, waits for them, and re-layouts, local(): weighted.reshape(count_query, local_heads, head_width * half_width)  7.39 us
    dot_general x1, matrix products, local(): jnp.einsum('kzo,kzj->koj', received, lax.all_gather(query_projection_inpu...  7.02 us
  transfers between devices with their start and end apart: 2, of which 1 were waited for; matrix products, arithmetic and copies ran while one was open for 32% of the time, Pallas kernels for 0%

profile of v1, /device:TPU:0, one launch (start us, length us, event | category | flops | bytes accessed | tf_op | source)
XLA Modules:
  0.0 142.8 jit_solution(6079685378154641665)
XLA Ops:
  6.5 0.7 all-gather.2.cloned.1.call-update
  7.3 1.7 %bitcast_dynamic-update-slice_fusion.7 = bf16[8,1,257,480]{3,2,1,0:T(8,128)(2,1)} fusion(bf16[1,257,3840]{2,1,0:T(8,128)(2,1)} %param.12), kind=kLoop, calls=%fused_computation.17 | loop fusion | bytes 517056
  8.9 1.8 %bitcast_dynamic-update-slice_fusion.6 = bf16[8,1,257,480]{3,2,1,0:T(8,128)(2,1)} fusion(bf16[8,1,257,480]{3,2,1,0:T(8,128)(2,1)} %bitcast_dynamic-update-slice_fusion.7, bf16[1,257,3840]{2,1,0:T(8,128)(2,1)} %param.12), kind=kLoop, calls=%fused_computation.16 | loop fusion | bytes 540672
  10.8 1.8 %bitcast_dynamic-update-slice_fusion.5 = bf16[8,1,257,480]{3,2,1,0:T(8,128)(2,1)} fusion(bf16[8,1,257,480]{3,2,1,0:T(8,128)(2,1)} %bitcast_dynamic-update-slice_fusion.6, bf16[1,257,3840]{2,1,0:T(8,128)(2,1)} %param.12), kind=kLoop, calls=%fused_computation.15 | loop fusion | bytes 540672
  12.6 1.8 %bitcast_dynamic-update-slice_fusion.4 = bf16[8,1,257,480]{3,2,1,0:T(8,128)(2,1)} fusion(bf16[8,1,257,480]{3,2,1,0:T(8,128)(2,1)} %bitcast_dynamic-update-slice_fusion.5, bf16[1,257,3840]{2,1,0:T(8,128)(2,1)} %param.12), kind=kLoop, calls=%fused_computation.14 | loop fusion | bytes 540672
  14.4 0.7 bitcast_dynamic-update-slice_fusion.3
  15.2 0.9 bitcast_dynamic-update-slice_fusion.2
  16.0 0.9 bitcast_dynamic-update-slice_fusion.1
  16.9 0.9 bitcast_dynamic-update-slice_fusion
  17.8 6.5 %all-to-all-start = ((bf16[8,1,257,480]{3,2,1,0:T(8,128)(2,1)}), bf16[8,1,257,480]{3,2,1,0:T(8,128)(2,1)S(1)}, u32[]{:S(2)}, u32[]{:S(2)}) async-start(bf16[8,1,257,480]{3,2,1,0:T(8,128)(2,1)} %bitcast_dynamic-update-slice_fusion), calls=%async_computation | async-start | bytes 4325376 | tf_op jit(solution)/shard_map/all_to_all | solution.py:18
  24.4 0.1 broadcast_in_dim.25
  24.5 0.3 select_reduce_fusion
  24.8 0.1 convert_element_type.36
  24.9 15.7 %convolution_convert_fusion = bf16[22,480,640]{2,1,0:T(8,128)(2,1)} fusion(bf16[22,257,480]{2,1,0:T(8,128)(2,1)} %param.9, bf16[22,257,640]{2,1,0:T(8,128)(2,1)} %param.8), kind=kOutput, calls=%fused_computation.2 | convolution fusion | flops 3480576000 | bytes 26181760 | tf_op jit(solution)/shard_map/nsr,nsd->nrd/dot_general | solution.py:48
  40.6 18.1 %reshape.38 = bf16[22,2,153600]{2,1,0:T(2,128)(2,1)} reshape(bf16[22,480,640]{2,1,0:T(8,128)(2,1)} %convolution_convert_fusion) | data formatting | bytes 27033600 | tf_op jit(solution)/shard_map/reshape | solution.py:61
  58.7 0.6 dynamic-slice
  60.0 31.2 %all-to-all-done = bf16[8,1,257,480]{3,2,1,0:T(8,128)(2,1)S(1)} async-done(((bf16[8,1,257,480]{3,2,1,0:T(8,128)(2,1)}), bf16[8,1,257,480]{3,2,1,0:T(8,128)(2,1)S(1)}, u32[]{:S(2)}, u32[]{:S(2)}) %all-to-all-start) | async-done | bytes 1973792 | tf_op jit(solution)/shard_map/all_to_all | solution.py:18
  91.2 7.0 %multiply_convert_fusion = bf16[8,480,640]{2,1,0:T(8,128)(2,1)} fusion(f32[480,640]{1,0:T(8,128)S(1)} %convert_element_type.36, bf16[8,257,640]{2,1,0:T(8,128)(2,1)} %all-gather.2.cloned.1.call-done, bf16[8,1,257,480]{3,2,1,0:T(8,128)(2,1)S(1)} %all-to-all-done), kind=kOutput, calls=%fused_computation.3 | convolution fusion | flops 1268121600 | bytes 10749440 | tf_op jit(solution)/shard_map/kzo,kzj->koj/dot_general | solution.py:53
  98.2 7.4 %reshape.40 = bf16[8,2,153600]{2,1,0:T(2,128)(2,1)} reshape(bf16[8,480,640]{2,1,0:T(8,128)(2,1)} %multiply_convert_fusion) | data formatting | bytes 9830400 | tf_op jit(solution)/shard_map/reshape | solution.py:62
  105.6 13.4 %fusion.4 = f32[2,22,8]{2,1,0:T(8,128)S(1)} fusion(bf16[8,2,153600]{2,1,0:T(2,128)(2,1)} %reshape.40, bf16[22,2,153600]{2,1,0:T(2,128)(2,1)} %reshape.38), kind=kOutput, calls=%fused_computation.7 | convolution fusion | flops 108134752 | bytes 18433408 | tf_op jit(solution)/shard_map/dot_general | solution.py:64
  118.9 0.2 fusion.10
  119.2 0.2 convolution_bitcast_fusion
  119.4 16.0 %all-reduce = f32[2,16,16]{2,1,0:T(8,128)S(1)} all-reduce(f32[2,16,16]{2,1,0:T(8,128)S(1)} %convolution_bitcast_fusion), channel_id=2, replica_groups=mesh['dp'=2,'tensor'=8,'fisher'=2] {'dp','fisher'}, use_global_device_ids=true, to_apply=%region_1.2.clone | all-reduce | flops 512 | bytes 4096
  135.4 0.6 copy.10
  (18 shorter events, 0.2 us)
Async XLA Ops:
  6.5 7.9 %copy-start = (bf16[1,257,3840]{2,1,0:T(8,128)(2,1)S(1)}, bf16[1,257,3840]{2,1,0:T(8,128)(2,1)}, u32[]{:S(2)}) copy-start(bf16[1,257,3840]{2,1,0:T(8,128)(2,1)} %param.12) | copy-start | bytes 5921284
  6.5 84.6 %all-gather.2.cloned.1.call-start = ((), (), s32[]{:S(2)}) async-start(), calls=%async_computation.1 | async-start | bytes 3041280 | tf_op jit(solution)/shard_map/all_gather | solution.py:56
  17.8 6.5 %copy-start.2 = (s32[16]{0:T(128)S(1)}, s32[16]{0:T(128)}, u32[]{:S(2)}) copy-start(s32[16]{0:T(128)} %param.15) | copy-start | bytes 196
  17.8 6.7 %copy-start.1 = (bf16[2,480,640]{2,1,0:T(8,128)(2,1)S(1)}, bf16[2,480,640]{2,1,0:T(8,128)(2,1)}, u32[]{:S(2)}) copy-start(bf16[2,480,640]{2,1,0:T(8,128)(2,1)} %param.14) | copy-start | bytes 3686404
  17.8 73.4 %all-to-all-start = ((bf16[8,1,257,480]{3,2,1,0:T(8,128)(2,1)}), bf16[8,1,257,480]{3,2,1,0:T(8,128)(2,1)S(1)}, u32[]{:S(2)}, u32[]{:S(2)}) async-start(bf16[8,1,257,480]{3,2,1,0:T(8,128)(2,1)} %bitcast_dynamic-update-slice_fusion), calls=%async_computation | async-start | bytes 4325376 | tf_op jit(solution)/shard_map/all_to_all | solution.py:18
  40.6 18.2 %copy-start.5 = (u32[32]{0:T(128)S(1)}, u32[32]{0:T(128)}, u32[]{:S(2)}) copy-start(u32[32]{0:T(128)} %constant.20) | copy-start | bytes 388
  105.6 13.4 %copy-start.3 = (s32[22]{0:T(128)S(1)}, s32[22]{0:T(128)}, u32[]{:S(2)}) copy-start(s32[22]{0:T(128)} %param.10) | copy-start | bytes 268
  105.6 13.6 %copy-start.4 = (s32[8]{0:T(128)S(1)}, s32[8]{0:T(128)}, u32[]{:S(2)}) copy-start(s32[8]{0:T(128)} %param.13) | copy-start | bytes 100
Sparse Core Ops, SparseCore 0:
  9.0 53.5 all-gather.1
